TPU v7x, 32 devices: a whole 2x2x4 slice. The times are simulated.
32 devices in a mesh: survey: 2 (over x), sector: 16 (over z, y, core).
Axes of the slice: x: 2, y: 2, z: 4, core: 2. Of those that a mesh axis runs over, the one named last changes fastest.
Arguments:
- raw_pings: bfloat16 [32, 512, 2, 1024], P('survey', 'sector'), parts along dimension 0, may hold values from -6 to 6
- focus_matrix: bfloat16 [2, 2048, 512], replicated, may hold values from -0.25 to 0.25
- start_angle: int32 [32], P('survey'), parts along dimension 0, may hold values from 0 to 2047
- ping_count: int32 [32], P('survey'), parts along dimension 0, may hold values from 256 to 512, as said below
Outputs:
- coherence: float32 [32, 2048, 1024], P(('survey', 'sector')), parts along dimension 0
- interferogram: bfloat16 [32, 2, 2048, 1024], P(('survey', 'sector')), parts along dimension 0
There are 2 independent parts, one for each index of `survey`. A program takes and returns all parts, laid end to end along the dimension named above; an argument that names none is the same for every part. Nothing has to cross between parts.
Inputs may be any that keep to these rules, and one draw needn't show every extreme that they name: `ping_count`: every value lies between 256 and 512, and at least one sector holds all 512 pings.
All inputs are finite; a program needn't handle non-finite values.
Results may differ from a plain program's by a relative error of at most 0.0057.
Values may be sent and summed in bfloat16 or wider, within the bound.
No kernel may reach another device: no remote copies, remote signals or barrier semaphores. Data moves between devices by JAX's collectives and lax.ppermute only.
A program may use at most 192 MiB of HBM per device.

v0:
```python
import jax
import jax.numpy as jnp
from jax import lax
from jax.sharding import PartitionSpec as P

WIN = 9


def shifted(block, axis, distance):
    devices = range(lax.axis_size(axis))
    route = [((i - distance) % len(devices), i) for i in devices]
    return lax.ppermute(block, axis, route)


def focus_sector(raw, angle_step, valid_pings, stacked):
    pings_here = raw.shape[0]
    ranges_here = raw.shape[2]
    columns_count = stacked.shape[0] // 2
    ping_mask = (jnp.arange(pings_here, dtype=jnp.int32) < valid_pings).astype(jnp.bfloat16)
    masked = raw * ping_mask[:, None, None]
    product = jnp.dot(
        stacked, masked.reshape(pings_here, 2 * ranges_here), preferred_element_type=jnp.float32
    )
    product = product.reshape(2, columns_count, 2, ranges_here)
    real_part = product[0, :, 0] - product[1, :, 1]
    imag_part = product[0, :, 1] + product[1, :, 0]
    columns = jnp.arange(columns_count, dtype=jnp.int32)
    turn_index = angle_step * columns % columns_count
    phase_turn = 2.0 * jnp.pi / columns_count * turn_index.astype(jnp.float32)
    cosine = jnp.cos(phase_turn)[:, None]
    sine_part = jnp.sin(phase_turn)[:, None]
    mean_power = jnp.mean(real_part * real_part + imag_part * imag_part, axis=0)
    inverse_rms = lax.rsqrt(mean_power + 1e-06)
    turned_real = (real_part * cosine + imag_part * sine_part) * inverse_rms
    turned_imag = (imag_part * cosine - real_part * sine_part) * inverse_rms
    return jnp.stack([turned_real, turned_imag], axis=1).astype(jnp.bfloat16)


def window_sum(field, axis, span):
    half_span = span // 2
    length_axis = field.shape[axis]
    widths = [(0, 0)] * field.ndim
    widths[axis] = (half_span, half_span)
    padded = jnp.pad(field, widths)
    total = lax.slice_in_dim(padded, 0, length_axis, axis=axis)
    for offset in range(1, span):
        total = total + lax.slice_in_dim(padded, offset, offset + length_axis, axis=axis)
    return total


def compare(own_image, other_image, span):
    f_real = own_image[:, 0].astype(jnp.float32)
    f_imag = own_image[:, 1].astype(jnp.float32)
    g_real = other_image[:, 0].astype(jnp.float32)
    g_imag = other_image[:, 1].astype(jnp.float32)
    fields = jnp.stack(
        [
            f_real * g_real + f_imag * g_imag,
            f_imag * g_real - f_real * g_imag,
            f_real * f_real + f_imag * f_imag,
            g_real * g_real + g_imag * g_imag,
        ],
        axis=0,
    )
    looked = window_sum(window_sum(fields, 1, span), 2, span)
    magnitude = jnp.sqrt(looked[0] * looked[0] + looked[1] * looked[1])
    energy = jnp.sqrt(looked[2] * looked[3] + 1e-06)
    coherence = magnitude / energy
    interferogram = (looked[0:2] / float(span * span)).astype(jnp.bfloat16)
    return (coherence, interferogram)


def body(raw_pings, focus_matrix, start_angle, ping_count):
    stacked = focus_matrix.reshape(2 * focus_matrix.shape[1], focus_matrix.shape[2])
    position = lax.axis_index("sector")

    def prepare(pieces, sector):
        return focus_sector(pieces[0], start_angle[sector], ping_count[sector], stacked)[None]

    own_image = (lambda pieces: prepare(pieces, position))(
        lax.all_to_all(raw_pings, "sector", split_axis=0, concat_axis=1, tiled=True)
    )
    other_image = shifted(own_image, "sector", -1)
    coherence, interferogram = compare(own_image[0], other_image[0], WIN)
    return (coherence[None], interferogram[None])


def solution(mesh):
    return jax.shard_map(
        body,
        mesh=mesh,
        in_specs=(P("survey", "sector", None, None), P(), P("survey"), P("survey")),
        out_specs=(P(("survey", "sector"), None, None), P(("survey", "sector"), None, None, None)),
        check_vma=False,
    )
```

profile of v0, /device:TPU:0, one launch (start us, length us, event | category | flops | bytes accessed | tf_op | source)
XLA Modules:
  0.0 722.9 jit_solution(4973740520128592052)
XLA Ops:
  0.6 7.4 %all-to-all-start = ((bf16[16,32,2,1024]{3,2,1,0:T(2,128)(2,1)}), bf16[16,32,2,1024]{3,2,1,0:T(2,128)(2,1)S(1)}, u32[]{:S(2)}, u32[]{:S(2)}) async-start(bf16[16,32,2,1024]{3,2,1,0:T(2,128)(2,1)} %param.4), calls=%async_computation | async-start | bytes 4194304 | tf_op jit(solution)/shard_map/all_to_all | solution.py:81
  8.1 1.2 dynamic_slice.6
  9.3 1.2 dynamic_slice.7
  10.5 0.7 fusion.37
  11.2 0.7 fusion.38
  11.9 37.1 %all-to-all-done = bf16[16,32,2,1024]{3,2,1,0:T(2,128)(2,1)S(1)} async-done(((bf16[16,32,2,1024]{3,2,1,0:T(2,128)(2,1)}), bf16[16,32,2,1024]{3,2,1,0:T(2,128)(2,1)S(1)}, u32[]{:S(2)}, u32[]{:S(2)}) %all-to-all-start) | async-done | bytes 2097184 | tf_op jit(solution)/shard_map/all_to_all | solution.py:81
  49.0 1.9 broadcast_multiply_fusion
  50.9 0.6 copy.14
  51.5 17.5 %convolution_bitcast_fusion = f32[4096,2048]{0,1:T(8,128)} fusion(bf16[512,2048]{1,0:T(8,128)(2,1)S(1)} %bitcast.52, bf16[4096,512]{1,0:T(8,128)(2,1)} %bitcast.53), kind=kOutput, calls=%fused_computation.23 | convolution fusion | flops 8589934592 | bytes 39845888 | tf_op jit(solution)/shard_map/dot_general | solution.py:21
  69.0 42.6 %reshape.411 = f32[2,2048,2,1024]{1,0,3,2:T(2,128)} reshape(f32[4096,2048]{0,1:T(8,128)} %convolution_bitcast_fusion) | data formatting | bytes 67108864 | tf_op jit(solution)/shard_map/reshape | solution.py:24
  111.7 39.8 %fusion.42 = (f32[1,2048,1,1024]{1,0,3,2:T(1,128)}, f32[1,2048,1,1024]{1,0,3,2:T(1,128)}, f32[1,2048,1,1024]{1,0,3,2:T(1,128)}, f32[1,2048,1,1024]{1,0,3,2:T(1,128)}) fusion(f32[2,2048,2,1024]{1,0,3,2:T(2,128)} %reshape.411), kind=kLoop, calls=%fused_computation.80 | loop fusion | bytes 67108864 | tf_op jit(solution)/shard_map/slice | solution.py:25
  151.5 20.7 %copy.10 = f32[1,2048,1,1024]{3,1,2,0:T(8,128)} copy(f32[1,2048,1,1024]{1,0,3,2:T(1,128)} %get-tuple-element.10) | data formatting | bytes 16777216
  172.3 20.7 %copy.11 = f32[1,2048,1,1024]{3,1,2,0:T(8,128)} copy(f32[1,2048,1,1024]{1,0,3,2:T(1,128)} %get-tuple-element.8) | data formatting | bytes 16777216
  192.9 20.5 %copy.12 = f32[1,2048,1,1024]{3,1,2,0:T(8,128)} copy(f32[1,2048,1,1024]{1,0,3,2:T(1,128)} %get-tuple-element.9) | data formatting | bytes 16777216
  213.5 20.5 %copy.13 = f32[1,2048,1,1024]{3,1,2,0:T(8,128)} copy(f32[1,2048,1,1024]{1,0,3,2:T(1,128)} %get-tuple-element.11) | data formatting | bytes 16777216
  234.0 19.2 %add_reduce_fusion = (f32[1024]{0:T(1024)S(1)}, f32[1,2048,1,1024]{3,1,2,0:T(8,128)}, f32[1,2048,1,1024]{3,1,2,0:T(8,128)}) fusion(f32[1,2048,1,1024]{3,1,2,0:T(8,128)} %copy.12, f32[1,2048,1,1024]{3,1,2,0:T(8,128)} %copy.13, f32[1,2048,1,1024]{3,1,2,0:T(8,128)} %copy.10, f32[1,2048,1,1024]{3,1,2,0:T(8,128)} %copy.11), kind=kLoop, calls=%fused_computation.64 | loop fusion | flops 12581888 | bytes 50335744 | tf_op jit(solution)/shard_map/reduce_sum | solution.py:32
  253.3 8.6 %multiply_convert_fusion.1 = (bf16[1,2048,1,1024]{3,1,2,0:T(8,128)(2,1)S(1)}, bf16[1,2048,1,1024]{3,1,2,0:T(8,128)(2,1)}) fusion(f32[1,2048,1,1024]{3,1,2,0:T(8,128)} %get-tuple-element.6, f32[1,2048,1,1024]{3,1,2,0:T(8,128)} %get-tuple-element.7, f32[1024]{0:T(1024)S(1)} %add_rsqrt_fusion, f32[2048]{0:T(1024)S(1)} %get-tuple-element.17, ...), kind=kLoop, calls=%fused_computation.63 | loop fusion | flops 20971520 | bytes 25186304 | tf_op jit(solution)/shard_map/convert
  261.9 6.2 pad_maximum_fusion.1
  268.0 9.8 %collective-permute-start = (bf16[1,2048,2,1024]{3,1,2,0:T(8,128)(2,1)}, bf16[1,2048,2,1024]{3,1,2,0:T(8,128)(2,1)S(1)}, u32[]{:S(2)}, u32[]{:S(2)}) collective-permute-start(bf16[1,2048,2,1024]{3,1,2,0:T(8,128)(2,1)} %pad_maximum_fusion.1), channel_id=1, source_target_pairs={{1,0},{2,1},{3,2},{4,3},{5,4},{6,5},{7,6},{8,7},{9,8},{10,9},{11,1... | collective-permute-start | bytes 25165832 | tf_op jit(solution)/shard_map/ppermute | solution.py:12
  277.9 91.3 %collective-permute-done = bf16[1,2048,2,1024]{3,1,2,0:T(8,128)(2,1)S(1)} collective-permute-done((bf16[1,2048,2,1024]{3,1,2,0:T(8,128)(2,1)}, bf16[1,2048,2,1024]{3,1,2,0:T(8,128)(2,1)S(1)}, u32[]{:S(2)}, u32[]{:S(2)}) %collective-permute-start) | collective-permute-done | bytes 8388640 | tf_op jit(solution)/shard_map/ppermute | solution.py:12
  369.2 13.3 %fusion.14 = (f32[1,2048,1024]{2,1,0:T(8,128)}, bf16[2048,1,1024]{2,0,1:T(8,128)(2,1)S(1)}, bf16[2048,1,1024]{2,0,1:T(8,128)(2,1)}) fusion(bf16[2048,2,1024]{2,0,1:T(8,128)(2,1)S(1)} %bitcast.49, f32[1024]{0:T(1024)S(1)} %add_rsqrt_fusion, f32[2048]{0:T(1024)S(1)} %get-tuple-element.17, f32[1,2048,1,1024]{3,1,2,0:T(8,128)} %get-tuple-element.7, ...), kind=kLoop, calls=%fused_computation.37 | loop fusion | flops 35651584 | bytes 41963520 | tf_op jit(solution)/shard_map/add | solution.py:58
  382.5 11.1 %fusion.18 = (f32[1,2048,1024]{2,1,0:T(8,128)}, f32[1,2048,1024]{2,1,0:T(8,128)}, f32[1,2048,1024]{2,1,0:T(8,128)}) fusion(bf16[2048,1,1024]{2,0,1:T(8,128)(2,1)S(1)} %get-tuple-element.3, bf16[2048,1,1024]{2,0,1:T(8,128)(2,1)} %get-tuple-element.4, bf16[2048,2,1024]{2,0,1:T(8,128)(2,1)S(1)} %bitcast.50), kind=kLoop, calls=%fused_computation.41 | loop fusion | flops 27262976 | bytes 41943040 | tf_op jit(solution)/shard_map/sub | solution.py:59
  393.6 23.4 %pad_maximum_fusion = f32[4,2048,1024]{2,1,0:T(8,128)} fusion(f32[1,2048,1024]{2,1,0:T(8,128)} %get-tuple-element.15, f32[1,2048,1024]{2,1,0:T(8,128)} %get-tuple-element.16, f32[1,2048,1024]{2,1,0:T(8,128)} %get-tuple-element.14, f32[1,2048,1024]{2,1,0:T(8,128)} %get-tuple-element.2), kind=kLoop, calls=%fused_computation.16 | loop fusion | flops 25165824 | bytes 67108864 | tf_op jit(solution)/shard_map/stack | solution.py:56
  417.0 131.8 %slice_add_fusion = f32[4,2048,1024]{2,1,0:T(8,128)} fusion(f32[4,2048,1024]{2,1,0:T(8,128)} %pad_maximum_fusion), kind=kLoop, calls=%fused_computation.17 | loop fusion | flops 67108864 | bytes 67108864 | tf_op jit(solution)/shard_map/add | solution.py:47
  548.8 147.7 %fusion.7 = f32[4,2048,1024]{2,1,0:T(8,128)} fusion(f32[4,2048,1024]{2,1,0:T(8,128)} %slice_add_fusion), kind=kLoop, calls=%fused_computation.15 | loop fusion | flops 67108864 | bytes 67108864 | tf_op jit(solution)/shard_map/add | solution.py:47
  696.5 9.6 %fusion.19 = bf16[1,2,2048,1024]{3,2,1,0:T(8,128)(2,1)} fusion(f32[4,2048,1024]{2,1,0:T(8,128)} %fusion.7), kind=kLoop, calls=%fused_computation.42 | loop fusion | flops 8388608 | bytes 25165824 | tf_op jit(solution)/shard_map/broadcast_in_dim | solution.py:85
  706.1 16.7 %fusion.22 = f32[1,2048,1024]{2,1,0:T(8,128)} fusion(f32[4,2048,1024]{2,1,0:T(8,128)} %fusion.7), kind=kLoop, calls=%fused_computation.46 | loop fusion | flops 12582912 | bytes 41943040 | tf_op jit(solution)/shard_map/div | solution.py:68
  (1 shorter events, 0.0 us)
Async XLA Ops:
  0.6 48.4 %all-to-all-start = ((bf16[16,32,2,1024]{3,2,1,0:T(2,128)(2,1)}), bf16[16,32,2,1024]{3,2,1,0:T(2,128)(2,1)S(1)}, u32[]{:S(2)}, u32[]{:S(2)}) async-start(bf16[16,32,2,1024]{3,2,1,0:T(2,128)(2,1)} %param.4), calls=%async_computation | async-start | bytes 4194304 | tf_op jit(solution)/shard_map/all_to_all | solution.py:81
  268.0 101.1 %collective-permute-start = (bf16[1,2048,2,1024]{3,1,2,0:T(8,128)(2,1)}, bf16[1,2048,2,1024]{3,1,2,0:T(8,128)(2,1)S(1)}, u32[]{:S(2)}, u32[]{:S(2)}) collective-permute-start(bf16[1,2048,2,1024]{3,1,2,0:T(8,128)(2,1)} %pad_maximum_fusion.1), channel_id=1, source_target_pairs={{1,0},{2,1},{3,2},{4,3},{5,4},{6,5},{7,6},{8,7},{9,8},{10,9},{11,1... | collective-permute-start | bytes 25165832 | tf_op jit(solution)/shard_map/ppermute | solution.py:12
where the time goes:
time: 726 us; the launch traced here: 723 us
  other arithmetic  391 us (54%)
  local copies, waits for them, and re-layouts  168 us (23%)
  waiting for transfers between devices  128 us (18%)
  matrix products  17.5 us (2%)
  starting transfers between devices  17.3 us (2%)
    add x2, other arithmetic, window_sum(): total + lax.slice_in_dim(padded, offset, offset + length_axis, axis=axis)  280 us
    ppermute x1, waiting for transfers between devices, shifted(): return lax.ppermute(block, axis, route)  91.3 us
    unnamed x5, local copies, waits for them, and re-layouts  83.1 us
    reshape x1, local copies, waits for them, and re-layouts, focus_sector(): product = product.reshape(2, columns_count, 2, ranges_here)  42.6 us
    slice x1, local copies, waits for them, and re-layouts, focus_sector(): real_part = product[0, :, 0] - product[1, :, 1]  39.8 us
    all_to_all x1, waiting for transfers between devices, body(): lax.all_to_all(raw_pings, 'sector', split_axis=0, concat_axis=1, tiled=True)  37.1 us
    another operation x1, other arithmetic, compare(): jnp.stack([f_real * g_real + f_imag * g_imag, f_imag * g_real - f_real *...  23.4 us
    reduce_sum x1, other arithmetic, focus_sector(): mean_power = jnp.mean(real_part * real_part + imag_part * imag_part, axis=0)  19.2 us
  transfers between devices with their start and end apart: 2, of which 2 were waited for; matrix products, arithmetic and copies ran while one was open for 1% of the time, Pallas kernels for 0%

commit v1 on v0

--- a/solution.py
+++ b/solution.py
@@ -4,6 +4,29 @@
 from jax.sharding import PartitionSpec as P
 
 WIN = 9
+
+
+def in_blocks(shard, dim, count):
+    before, after = (shard.shape[:dim], shard.shape[dim + 1 :])
+    return jnp.moveaxis(shard.reshape(*before, count, -1, *after), dim, 0)
+
+
+def in_order(pieces, dim):
+    pieces = jnp.moveaxis(pieces, 0, dim)
+    lengths = pieces.shape
+    return pieces.reshape(*lengths[:dim], lengths[dim] * lengths[dim + 1], *lengths[dim + 2 :])
+
+
+def exchange_directly(array, axis, split_dim, concat_dim):
+    length, here = (lax.axis_size(axis), lax.axis_index(axis))
+    blocks = in_blocks(array, split_dim, length)
+    out = blocks
+    for step in range(1, length):
+        target, source = ((here + step) % length, (here - step) % length)
+        sent = lax.dynamic_index_in_dim(blocks, target, 0)
+        received = lax.ppermute(sent, axis, [(i, (i + step) % length) for i in range(length)])
+        out = lax.dynamic_update_slice_in_dim(out, received, source, axis=0)
+    return in_order(out, concat_dim)
 
 
 def shifted(block, axis, distance):
@@ -78,7 +101,7 @@
         return focus_sector(pieces[0], start_angle[sector], ping_count[sector], stacked)[None]
 
     own_image = (lambda pieces: prepare(pieces, position))(
-        lax.all_to_all(raw_pings, "sector", split_axis=0, concat_axis=1, tiled=True)
+        exchange_directly(raw_pings, "sector", 0, 1)
     )
     other_image = shifted(own_image, "sector", -1)
     coherence, interferogram = compare(own_image[0], other_image[0], WIN)

time: 726 us -> 737 us (1.015)
  waiting for transfers between devices: 128 us -> 105 us
  starting transfers between devices: 17.3 us -> 35.2 us
  local copies, waits for them, and re-layouts: 168 us -> 178 us
    all_to_all x1 -> x0, waiting for transfers between devices: 37.1 us -> none  [body(): lax.all_to_all(raw_pings, 'sector', split_axis=0, concat_axis=1, tiled=True)]
    ppermute x0 -> x15, starting transfers between devices: none -> 30.6 us  [exchange_directly(): lax.ppermute(sent, axis, [(i, (i + step) % length) for i in range(length)])]
    ppermute x0 -> x15, waiting for transfers between devices: none -> 13.4 us  [exchange_directly(): lax.ppermute(sent, axis, [(i, (i + step) % length) for i in range(length)])]
    all_to_all x1 -> x0, starting transfers between devices: 7.43 us -> none  [body(): lax.all_to_all(raw_pings, 'sector', split_axis=0, concat_axis=1, tiled=True)]
    unnamed x5 -> x8, local copies, waits for them, and re-layouts: 83.1 us -> 84.8 us
  transfers between devices with their start and end apart: 2 -> 16, of which waited for: 2 -> 4; matrix products, arithmetic and copies ran while one was open for 1% -> 1% of each run, Pallas kernels for 0% -> 0%
where the time goes in v1:
time: 737 us; the launch traced here: 727 us
  other arithmetic  391 us (53%)
  local copies, waits for them, and re-layouts  178 us (24%)
  waiting for transfers between devices  105 us (14%)
  starting transfers between devices  35.2 us (5%)
  matrix products  18 us (2%)
    add x2, other arithmetic, window_sum(): total + lax.slice_in_dim(padded, offset, offset + length_axis, axis=axis)  278 us
    ppermute x1, waiting for transfers between devices, shifted(): return lax.ppermute(block, axis, route)  91.3 us
    unnamed x8, local copies, waits for them, and re-layouts  84.8 us
    reshape x1, local copies, waits for them, and re-layouts, focus_sector(): product = product.reshape(2, columns_count, 2, ranges_here)  42.6 us
    slice x1, local copies, waits for them, and re-layouts, focus_sector(): real_part = product[0, :, 0] - product[1, :, 1]  39.7 us
    ppermute x15, starting transfers between devices, exchange_directly(): lax.ppermute(sent, axis, [(i, (i + step) % length) for i in range(length)])  30.6 us
    another operation x1, other arithmetic, compare(): jnp.stack([f_real * g_real + f_imag * g_imag, f_imag * g_real - f_real *...  23.5 us
    reduce_sum x1, other arithmetic, focus_sector(): mean_power = jnp.mean(real_part * real_part + imag_part * imag_part, axis=0)  19.1 us
  transfers between devices with their start and end apart: 16, of which 4 were waited for; matrix products, arithmetic and copies ran while one was open for 1% of the time, Pallas kernels for 0%

profile of v1, /device:TPU:0, one launch (start us, length us, event | category | flops | bytes accessed | tf_op | source)
XLA Modules:
  0.0 727.5 jit_solution(1112271260539730422)
XLA Ops:
  0.6 1.6 copy.31
  2.2 2.5 dynamic-slice_bitcast_fusion
  4.8 0.5 collective-permute-start
  5.3 2.5 collective-permute-start.1
  7.8 2.5 collective-permute-start.2
  10.3 1.6 collective-permute-start.3
  11.8 0.1 collective-permute-start.4
  11.9 0.6 dynamic_slice.68
  12.5 0.6 fusion.38
  13.2 1.3 dynamic_slice.67
  14.5 1.3 fusion.37
  15.8 1.2 collective-permute-start.5
  16.9 1.0 constant_dynamic-update-slice_fusion.14
  18.0 4.4 collective-permute-start.6
  22.4 1.0 constant_dynamic-update-slice_fusion.13
  23.4 0.4 collective-permute-start.7
  23.8 1.0 constant_dynamic-update-slice_fusion.12
  24.8 0.3 collective-permute-start.8
  25.1 1.0 constant_dynamic-update-slice_fusion.11
  26.1 10.9 %collective-permute-done.4 = bf16[1,1,32,2,1024]{4,3,2,0,1:T(2,128)(2,1)} collective-permute-done((bf16[1,1,32,2,1024]{4,3,2,0,1:T(2,128)(2,1)S(1)}, bf16[1,1,32,2,1024]{4,3,2,0,1:T(2,128)(2,1)}, u32[]{:S(2)}, u32[]{:S(2)}) %collective-permute-start.4) | collective-permute-done | bytes 131104 | tf_op jit(solution)/shard_map/ppermute | solution.py:27
  37.0 1.0 constant_dynamic-update-slice_fusion.10
  38.0 3.0 collective-permute-start.10
  41.1 5.3 collective-permute-start.11
  46.5 1.2 collective-permute-start.12
  47.8 4.7 collective-permute-start.13
  52.6 2.9 collective-permute-start.14
  56.0 2.4 collective-permute-done.13
  58.8 2.6 broadcast_multiply_fusion
  61.4 0.6 copy.14
  62.0 18.0 %convolution_bitcast_fusion = f32[4096,2048]{0,1:T(8,128)} fusion(bf16[512,2048]{1,0:T(8,128)(2,1)S(1)} %bitcast.85, bf16[4096,512]{1,0:T(8,128)(2,1)} %bitcast.86), kind=kOutput, calls=%fused_computation.23 | convolution fusion | flops 8589934592 | bytes 39845888 | tf_op jit(solution)/shard_map/dot_general | solution.py:44
  80.0 42.6 %reshape.425 = f32[2,2048,2,1024]{1,0,3,2:T(2,128)} reshape(f32[4096,2048]{0,1:T(8,128)} %convolution_bitcast_fusion) | data formatting | bytes 67108864 | tf_op jit(solution)/shard_map/reshape | solution.py:47
  122.6 39.7 %fusion.42 = (f32[1,2048,1,1024]{1,0,3,2:T(1,128)}, f32[1,2048,1,1024]{1,0,3,2:T(1,128)}, f32[1,2048,1,1024]{1,0,3,2:T(1,128)}, f32[1,2048,1,1024]{1,0,3,2:T(1,128)}) fusion(f32[2,2048,2,1024]{1,0,3,2:T(2,128)} %reshape.425), kind=kLoop, calls=%fused_computation.110 | loop fusion | bytes 67108864 | tf_op jit(solution)/shard_map/slice | solution.py:48
  162.4 20.8 %copy.10 = f32[1,2048,1,1024]{3,1,2,0:T(8,128)} copy(f32[1,2048,1,1024]{1,0,3,2:T(1,128)} %get-tuple-element.10) | data formatting | bytes 16777216
  183.2 20.7 %copy.11 = f32[1,2048,1,1024]{3,1,2,0:T(8,128)} copy(f32[1,2048,1,1024]{1,0,3,2:T(1,128)} %get-tuple-element.8) | data formatting | bytes 16777216
  203.9 20.5 %copy.12 = f32[1,2048,1,1024]{3,1,2,0:T(8,128)} copy(f32[1,2048,1,1024]{1,0,3,2:T(1,128)} %get-tuple-element.9) | data formatting | bytes 16777216
  224.4 20.5 %copy.13 = f32[1,2048,1,1024]{3,1,2,0:T(8,128)} copy(f32[1,2048,1,1024]{1,0,3,2:T(1,128)} %get-tuple-element.11) | data formatting | bytes 16777216
  245.0 19.1 %add_reduce_fusion = (f32[1024]{0:T(1024)S(1)}, f32[1,2048,1,1024]{3,1,2,0:T(8,128)}, f32[1,2048,1,1024]{3,1,2,0:T(8,128)}) fusion(f32[1,2048,1,1024]{3,1,2,0:T(8,128)} %copy.12, f32[1,2048,1,1024]{3,1,2,0:T(8,128)} %copy.13, f32[1,2048,1,1024]{3,1,2,0:T(8,128)} %copy.10, f32[1,2048,1,1024]{3,1,2,0:T(8,128)} %copy.11), kind=kLoop, calls=%fused_computation.64 | loop fusion | flops 12581888 | bytes 50335744 | tf_op jit(solution)/shard_map/reduce_sum | solution.py:55
  264.1 8.7 %multiply_convert_fusion.1 = (bf16[1,2048,1,1024]{3,1,2,0:T(8,128)(2,1)S(1)}, bf16[1,2048,1,1024]{3,1,2,0:T(8,128)(2,1)}) fusion(f32[1,2048,1,1024]{3,1,2,0:T(8,128)} %get-tuple-element.6, f32[1,2048,1,1024]{3,1,2,0:T(8,128)} %get-tuple-element.7, f32[1024]{0:T(1024)S(1)} %add_rsqrt_fusion, f32[2048]{0:T(1024)S(1)} %get-tuple-element.32, ...), kind=kLoop, calls=%fused_computation.63 | loop fusion | flops 20971520 | bytes 25186304 | tf_op jit(solution)/shard_map/convert
  272.8 6.2 pad_maximum_fusion.1
  279.0 4.6 collective-permute-start.15
  283.6 91.3 %collective-permute-done.15 = bf16[1,2048,2,1024]{3,1,2,0:T(8,128)(2,1)S(1)} collective-permute-done((bf16[1,2048,2,1024]{3,1,2,0:T(8,128)(2,1)}, bf16[1,2048,2,1024]{3,1,2,0:T(8,128)(2,1)S(1)}, u32[]{:S(2)}, u32[]{:S(2)}) %collective-permute-start.15) | collective-permute-done | bytes 8388640 | tf_op jit(solution)/shard_map/ppermute | solution.py:35
  374.9 13.3 %fusion.14 = (f32[1,2048,1024]{2,1,0:T(8,128)}, bf16[2048,1,1024]{2,0,1:T(8,128)(2,1)S(1)}, bf16[2048,1,1024]{2,0,1:T(8,128)(2,1)}) fusion(bf16[2048,2,1024]{2,0,1:T(8,128)(2,1)S(1)} %bitcast.81, f32[1024]{0:T(1024)S(1)} %add_rsqrt_fusion, f32[2048]{0:T(1024)S(1)} %get-tuple-element.32, f32[1,2048,1,1024]{3,1,2,0:T(8,128)} %get-tuple-element.7, ...), kind=kLoop, calls=%fused_computation.37 | loop fusion | flops 35651584 | bytes 41963520 | tf_op jit(solution)/shard_map/add | solution.py:81
  388.2 11.1 %fusion.18 = (f32[1,2048,1024]{2,1,0:T(8,128)}, f32[1,2048,1024]{2,1,0:T(8,128)}, f32[1,2048,1024]{2,1,0:T(8,128)}) fusion(bf16[2048,1,1024]{2,0,1:T(8,128)(2,1)S(1)} %get-tuple-element.3, bf16[2048,1,1024]{2,0,1:T(8,128)(2,1)} %get-tuple-element.4, bf16[2048,2,1024]{2,0,1:T(8,128)(2,1)S(1)} %bitcast.82), kind=kLoop, calls=%fused_computation.41 | loop fusion | flops 27262976 | bytes 41943040 | tf_op jit(solution)/shard_map/sub | solution.py:82
  399.3 23.5 %pad_maximum_fusion = f32[4,2048,1024]{2,1,0:T(8,128)} fusion(f32[1,2048,1024]{2,1,0:T(8,128)} %get-tuple-element.15, f32[1,2048,1024]{2,1,0:T(8,128)} %get-tuple-element.16, f32[1,2048,1024]{2,1,0:T(8,128)} %get-tuple-element.14, f32[1,2048,1024]{2,1,0:T(8,128)} %get-tuple-element.2), kind=kLoop, calls=%fused_computation.16 | loop fusion | flops 25165824 | bytes 67108864 | tf_op jit(solution)/shard_map/stack | solution.py:79
  422.8 131.1 %slice_add_fusion = f32[4,2048,1024]{2,1,0:T(8,128)} fusion(f32[4,2048,1024]{2,1,0:T(8,128)} %pad_maximum_fusion), kind=kLoop, calls=%fused_computation.17 | loop fusion | flops 67108864 | bytes 67108864 | tf_op jit(solution)/shard_map/add | solution.py:70
  553.9 147.0 %fusion.7 = f32[4,2048,1024]{2,1,0:T(8,128)} fusion(f32[4,2048,1024]{2,1,0:T(8,128)} %slice_add_fusion), kind=kLoop, calls=%fused_computation.15 | loop fusion | flops 67108864 | bytes 67108864 | tf_op jit(solution)/shard_map/add | solution.py:70
  700.9 9.6 %fusion.19 = bf16[1,2,2048,1024]{3,2,1,0:T(8,128)(2,1)} fusion(f32[4,2048,1024]{2,1,0:T(8,128)} %fusion.7), kind=kLoop, calls=%fused_computation.42 | loop fusion | flops 8388608 | bytes 25165824 | tf_op jit(solution)/shard_map/broadcast_in_dim | solution.py:108
  710.5 16.7 %fusion.22 = f32[1,2048,1024]{2,1,0:T(8,128)} fusion(f32[4,2048,1024]{2,1,0:T(8,128)} %fusion.7), kind=kLoop, calls=%fused_computation.46 | loop fusion | flops 12582912 | bytes 41943040 | tf_op jit(solution)/shard_map/div | solution.py:91
  (27 shorter events, 1.2 us)
Async XLA Ops:
  0.6 11.3 %copy-start = (s32[16]{0:T(128)S(1)}, s32[16]{0:T(128)}, u32[]{:S(2)}) copy-start(s32[16]{0:T(128)} %param.6) | copy-start | bytes 196
  4.8 11.0 %collective-permute-start = (bf16[1,1,32,2,1024]{4,3,2,0,1:T(2,128)(2,1)}, bf16[1,1,32,2,1024]{4,3,2,0,1:T(2,128)(2,1)}, u32[]{:S(2)}, u32[]{:S(2)}) collective-permute-start(bf16[1,1,32,2,1024]{4,3,2,0,1:T(2,128)(2,1)} %get-tuple-element.30), channel_id=1, source_target_pairs={{0,1},{1,2},{2,3},{3,4},{4,5},{5,6},{6,7},{7,8},{8,9},{9,10},{10,1... | collective-permute-start | bytes 393224 | tf_op jit(solution)/shard_map/ppermute | solution.py:27
  5.3 12.7 %collective-permute-start.1 = (bf16[1,1,32,2,1024]{4,3,2,0,1:T(2,128)(2,1)}, bf16[1,1,32,2,1024]{4,3,2,0,1:T(2,128)(2,1)}, u32[]{:S(2)}, u32[]{:S(2)}) collective-permute-start(bf16[1,1,32,2,1024]{4,3,2,0,1:T(2,128)(2,1)} %get-tuple-element.29), channel_id=1, source_target_pairs={{0,2},{1,3},{2,4},{3,5},{4,6},{5,7},{6,8},{7,9},{8,10},{9,11},{10,... | collective-permute-start | bytes 393224 | tf_op jit(solution)/shard_map/ppermute | solution.py:27
  7.8 15.6 %collective-permute-start.2 = (bf16[1,1,32,2,1024]{4,3,2,0,1:T(2,128)(2,1)}, bf16[1,1,32,2,1024]{4,3,2,0,1:T(2,128)(2,1)}, u32[]{:S(2)}, u32[]{:S(2)}) collective-permute-start(bf16[1,1,32,2,1024]{4,3,2,0,1:T(2,128)(2,1)} %get-tuple-element.28), channel_id=1, source_target_pairs={{0,3},{1,4},{2,5},{3,6},{4,7},{5,8},{6,9},{7,10},{8,11},{9,12},{10... | collective-permute-start | bytes 393224 | tf_op jit(solution)/shard_map/ppermute | solution.py:27
  10.3 14.6 %collective-permute-start.3 = (bf16[1,1,32,2,1024]{4,3,2,0,1:T(2,128)(2,1)}, bf16[1,1,32,2,1024]{4,3,2,0,1:T(2,128)(2,1)}, u32[]{:S(2)}, u32[]{:S(2)}) collective-permute-start(bf16[1,1,32,2,1024]{4,3,2,0,1:T(2,128)(2,1)} %get-tuple-element.27), channel_id=1, source_target_pairs={{0,4},{1,5},{2,6},{3,7},{4,8},{5,9},{6,10},{7,11},{8,12},{9,13},{1... | collective-permute-start | bytes 393224 | tf_op jit(solution)/shard_map/ppermute | solution.py:27
  11.8 25.2 %collective-permute-start.4 = (bf16[1,1,32,2,1024]{4,3,2,0,1:T(2,128)(2,1)S(1)}, bf16[1,1,32,2,1024]{4,3,2,0,1:T(2,128)(2,1)}, u32[]{:S(2)}, u32[]{:S(2)}) collective-permute-start(bf16[1,1,32,2,1024]{4,3,2,0,1:T(2,128)(2,1)S(1)} %get-tuple-element.26), channel_id=1, source_target_pairs={{0,5},{1,6},{2,7},{3,8},{4,9},{5,10},{6,11},{7,12},{8,13},{9,14},{... | collective-permute-start | bytes 393224 | tf_op jit(solution)/shard_map/ppermute | solution.py:27
  15.8 22.2 %collective-permute-start.5 = (bf16[1,1,32,2,1024]{4,3,2,0,1:T(2,128)(2,1)S(1)}, bf16[1,1,32,2,1024]{4,3,2,0,1:T(2,128)(2,1)S(1)}, u32[]{:S(2)}, u32[]{:S(2)}) collective-permute-start(bf16[1,1,32,2,1024]{4,3,2,0,1:T(2,128)(2,1)S(1)} %get-tuple-element.25), channel_id=1, source_target_pairs={{0,6},{1,7},{2,8},{3,9},{4,10},{5,11},{6,12},{7,13},{8,14},{9,15},... | collective-permute-start | bytes 393224 | tf_op jit(solution)/shard_map/ppermute | solution.py:27
  18.0 23.1 %collective-permute-start.6 = (bf16[1,1,32,2,1024]{4,3,2,0,1:T(2,128)(2,1)S(1)}, bf16[1,1,32,2,1024]{4,3,2,0,1:T(2,128)(2,1)S(1)}, u32[]{:S(2)}, u32[]{:S(2)}) collective-permute-start(bf16[1,1,32,2,1024]{4,3,2,0,1:T(2,128)(2,1)S(1)} %get-tuple-element.24), channel_id=1, source_target_pairs={{0,7},{1,8},{2,9},{3,10},{4,11},{5,12},{6,13},{7,14},{8,15},{9,0},... | collective-permute-start | bytes 393224 | tf_op jit(solution)/shard_map/ppermute | solution.py:27
  23.4 23.1 %collective-permute-start.7 = (bf16[1,1,32,2,1024]{4,3,2,0,1:T(2,128)(2,1)S(1)}, bf16[1,1,32,2,1024]{4,3,2,0,1:T(2,128)(2,1)S(1)}, u32[]{:S(2)}, u32[]{:S(2)}) collective-permute-start(bf16[1,1,32,2,1024]{4,3,2,0,1:T(2,128)(2,1)S(1)} %get-tuple-element.23), channel_id=1, source_target_pairs={{0,8},{1,9},{2,10},{3,11},{4,12},{5,13},{6,14},{7,15},{8,0},{9,1},... | collective-permute-start | bytes 393224 | tf_op jit(solution)/shard_map/ppermute | solution.py:27
  24.8 23.0 %collective-permute-start.8 = (bf16[1,1,32,2,1024]{4,3,2,0,1:T(2,128)(2,1)S(1)}, bf16[1,1,32,2,1024]{4,3,2,0,1:T(2,128)(2,1)S(1)}, u32[]{:S(2)}, u32[]{:S(2)}) collective-permute-start(bf16[1,1,32,2,1024]{4,3,2,0,1:T(2,128)(2,1)S(1)} %get-tuple-element.22), channel_id=1, source_target_pairs={{0,9},{1,10},{2,11},{3,12},{4,13},{5,14},{6,15},{7,0},{8,1},{9,2},... | collective-permute-start | bytes 393224 | tf_op jit(solution)/shard_map/ppermute | solution.py:27
  37.0 15.6 %collective-permute-start.9 = (bf16[1,1,32,2,1024]{4,3,2,0,1:T(2,128)(2,1)S(1)}, bf16[1,1,32,2,1024]{4,3,2,0,1:T(2,128)(2,1)S(1)}, u32[]{:S(2)}, u32[]{:S(2)}) collective-permute-start(bf16[1,1,32,2,1024]{4,3,2,0,1:T(2,128)(2,1)S(1)} %get-tuple-element.21), channel_id=1, source_target_pairs={{0,10},{1,11},{2,12},{3,13},{4,14},{5,15},{6,0},{7,1},{8,2},{9,3},... | collective-permute-start | bytes 393224 | tf_op jit(solution)/shard_map/ppermute | solution.py:27
  38.0 17.7 %collective-permute-start.10 = (bf16[1,1,32,2,1024]{4,3,2,0,1:T(2,128)(2,1)S(1)}, bf16[1,1,32,2,1024]{4,3,2,0,1:T(2,128)(2,1)S(1)}, u32[]{:S(2)}, u32[]{:S(2)}) collective-permute-start(bf16[1,1,32,2,1024]{4,3,2,0,1:T(2,128)(2,1)S(1)} %get-tuple-element.20), channel_id=1, source_target_pairs={{0,11},{1,12},{2,13},{3,14},{4,15},{5,0},{6,1},{7,2},{8,3},{9,4},{... | collective-permute-start | bytes 393224 | tf_op jit(solution)/shard_map/ppermute | solution.py:27
  41.1 14.7 %collective-permute-start.11 = (bf16[1,1,32,2,1024]{4,3,2,0,1:T(2,128)(2,1)S(1)}, bf16[1,1,32,2,1024]{4,3,2,0,1:T(2,128)(2,1)S(1)}, u32[]{:S(2)}, u32[]{:S(2)}) collective-permute-start(bf16[1,1,32,2,1024]{4,3,2,0,1:T(2,128)(2,1)S(1)} %get-tuple-element.19), channel_id=1, source_target_pairs={{0,12},{1,13},{2,14},{3,15},{4,0},{5,1},{6,2},{7,3},{8,4},{9,5},{1... | collective-permute-start | bytes 393224 | tf_op jit(solution)/shard_map/ppermute | solution.py:27
  46.5 9.4 %collective-permute-start.12 = (bf16[1,1,32,2,1024]{4,3,2,0,1:T(2,128)(2,1)S(1)}, bf16[1,1,32,2,1024]{4,3,2,0,1:T(2,128)(2,1)S(1)}, u32[]{:S(2)}, u32[]{:S(2)}) collective-permute-start(bf16[1,1,32,2,1024]{4,3,2,0,1:T(2,128)(2,1)S(1)} %get-tuple-element.18), channel_id=1, source_target_pairs={{0,13},{1,14},{2,15},{3,0},{4,1},{5,2},{6,3},{7,4},{8,5},{9,6},{10... | collective-permute-start | bytes 393224 | tf_op jit(solution)/shard_map/ppermute | solution.py:27
  47.8 10.7 %collective-permute-start.13 = (bf16[1,1,32,2,1024]{4,3,2,0,1:T(2,128)(2,1)S(1)}, bf16[1,1,32,2,1024]{4,3,2,0,1:T(2,128)(2,1)S(1)}, u32[]{:S(2)}, u32[]{:S(2)}) collective-permute-start(bf16[1,1,32,2,1024]{4,3,2,0,1:T(2,128)(2,1)S(1)} %get-tuple-element.31), channel_id=1, source_target_pairs={{0,14},{1,15},{2,0},{3,1},{4,2},{5,3},{6,4},{7,5},{8,6},{9,7},{10,... | collective-permute-start | bytes 393224 | tf_op jit(solution)/shard_map/ppermute | solution.py:27
  52.6 6.1 collective-permute-start.14
  279.0 95.9 %collective-permute-start.15 = (bf16[1,2048,2,1024]{3,1,2,0:T(8,128)(2,1)}, bf16[1,2048,2,1024]{3,1,2,0:T(8,128)(2,1)S(1)}, u32[]{:S(2)}, u32[]{:S(2)}) collective-permute-start(bf16[1,2048,2,1024]{3,1,2,0:T(8,128)(2,1)} %pad_maximum_fusion.1), channel_id=1, source_target_pairs={{1,0},{2,1},{3,2},{4,3},{5,4},{6,5},{7,6},{8,7},{9,8},{10,9},{11,1... | collective-permute-start | bytes 25165832 | tf_op jit(solution)/shard_map/ppermute | solution.py:35
